TPU v7x, 512 devices: a whole 4x8x8 slice. The times are simulated.
512 devices in a mesh: date: 16 (over z, x_hi), trade: 16 (over y, core), path: 2 (over x_lo).
Axes of the slice: x: 4 (x_hi: 2, x_lo: 2; x = x_hi * 2 + x_lo), y: 8, z: 8, core: 2. Of those that a mesh axis runs over, the one named last changes fastest.
Arguments:
- normals: bfloat16 [32, 64, 8192], P('date', None, ('trade', 'path')), may hold values from -6 to 6
- chol: float32 [64, 64], replicated, as said below
- volatility: float32 [64], replicated, may hold values from 0.5 to 2
- start_state: float32 [64], replicated, may hold values from -3 to 3
- basis_map: float32 [64, 128], replicated, may hold values from -0.75 to 0.75
- basis_bias: float32 [128], replicated, may hold values from -3 to 3
- coef: bfloat16 [128, 16384], P(None, 'trade'), may hold values from -0.5 to 0.5
- maturity: int32 [16384], P('trade'), may hold values from 1 to 32
- netting: int32 [16384], P('trade'), may hold values from 0 to 2047, as said below
Outputs:
- exposure: float32 [32, 2048], P('date', 'trade')
Inputs may be any that keep to these rules, and one draw needn't show every extreme that they name: netting sets are whole within a shard of trades: netting[j] // 128 == j // 1024, and every netting set holds at least one trade. `chol`: lower triangular with a positive diagonal.
All inputs are finite; a program needn't handle non-finite values.
Results may differ from a plain program's by a relative error of at most 0.00035.
Values may be sent and summed in bfloat16 or wider, within the bound.
A program may use at most 64 MiB of HBM per device.

v0:
```python
import jax
import jax.numpy as jnp
from jax import lax
from jax.sharding import PartitionSpec as P

NS_DEV = 128


def entering(array, axis, join, neutral):
    place = lax.axis_index(axis)
    gathered = lax.all_gather(array.astype(jnp.bfloat16), axis)
    state = jnp.zeros_like(array) + jnp.asarray(neutral, array.dtype)

    def one(lap, state):
        return join(state, lax.dynamic_index_in_dim(gathered, lap, 0, False).astype(array.dtype))

    return lax.fori_loop(0, place, one, state)


def add_pair(earlier, later):
    return earlier + later


def local_moves(draws, chol, volatility, date_total):
    scale = volatility * jnp.sqrt(jnp.float32(1.0) / date_total)
    moves = jnp.einsum(
        "fg,tgp->tfp", chol, draws.astype(jnp.float32), precision=lax.Precision.HIGHEST
    )
    return jnp.cumsum(moves * scale[None, :, None], axis=0)


def shards(normals, chol, volatility, start_state, basis_map, basis_bias, coef, maturity, netting):
    date_count, factor_count, path_count = normals.shape
    trade_count = coef.shape[1]
    set_count = trade_count * 0 + NS_DEV
    date_total = date_count * lax.axis_size("date")
    path_total = path_count * lax.axis_size("trade") * lax.axis_size("path")
    first_date = lax.axis_index("date") * date_count
    when = first_date + jnp.arange(date_count, dtype=jnp.int32)
    alive = (when[:, None] < maturity[None, :]).astype(jnp.float32)
    local_set = netting - lax.axis_index("trade") * set_count
    member = (local_set[:, None] == jnp.arange(set_count, dtype=jnp.int32)[None, :]).astype(
        jnp.bfloat16
    )
    own_local = local_moves(normals, chol, volatility, date_total)
    empty = jnp.zeros_like(own_local[-1])
    prior = entering(own_local[-1], "date", add_pair, empty)
    states = start_state[None, :, None] + prior[None] + own_local
    pre = jnp.einsum(
        "tfp,fk->tpk",
        lax.all_gather(states, "trade", axis=2, tiled=True),
        basis_map,
        precision=lax.Precision.HIGHEST,
    )
    basis = jnp.tanh(pre + basis_bias[None, None, :]).astype(jnp.bfloat16)
    value = jnp.einsum("tpk,kj->tpj", basis, coef, preferred_element_type=jnp.float32)
    value = (value * alive[:, None, :]).astype(jnp.bfloat16)
    net = jnp.einsum("tpj,js->tps", value, member, preferred_element_type=jnp.float32)
    total = jnp.sum(jnp.maximum(net, 0.0), axis=1)
    summed = lax.psum(total, "path")
    return summed / path_total


def solution(mesh):
    placed = (
        P("date", None, ("trade", "path")),
        P(),
        P(),
        P(),
        P(),
        P(),
        P(None, "trade"),
        P("trade"),
        P("trade"),
    )
    return jax.shard_map(
        shards, mesh=mesh, in_specs=placed, out_specs=P("date", "trade"), check_vma=False
    )
```

profile of v0, /device:TPU:1, one launch (start us, length us, event | category | flops | bytes accessed | tf_op | source)
XLA Modules:
  0.0 125.8 jit_solution(15111759457493451321)
XLA Ops:
  6.5 0.0 copy-start
  6.5 0.0 copy-start.4
  6.5 0.0 copy-start.3
  6.5 0.0 copy-start.2
  6.5 0.0 copy-start.1
  6.5 0.0 copy-start.5
  6.6 0.0 all-gather.2.cloned.1.call-start
  6.6 0.7 broadcast_multiply_fusion.1
  7.3 1.0 fusion.8
  8.4 0.1 fusion.16
  8.5 43.9 %all_gather.7 = bf16[16,64,256]{2,1,0:T(8,128)(2,1)S(1)} all-gather(bf16[1,64,256]{2,1,0:T(8,128)(2,1)S(1)} %slice.7), channel_id=1, replica_groups=mesh['date'=16,'trade'=16,'path'=2] {'date'}, dimensions={0}, use_global_device_ids=true | all-gather | bytes 557056 | tf_op jit(solution)/shard_map/all_gather | solution.py:11
  52.4 0.0 copy-done.4
  52.4 0.1 broadcast_add_fusion.1
  52.5 0.7 broadcast_add_fusion
  53.2 0.0 all-gather.2.cloned.1.call-update
  53.2 0.0 copy-done.3
  53.2 0.0 copy-done.2
  53.2 0.1 compare_convert_fusion
  53.3 43.9 %all-gather.2.cloned.1.call-done = f32[2,64,4096]{2,1,0:T(8,128)} async-done(((f32[2,64,256]{2,1,0:T(8,128)}), f32[2,64,4096]{2,1,0:T(8,128)}) %all-gather.2.cloned.1.call-update) | async-done | bytes 2097168 | tf_op jit(solution)/shard_map/all_gather | solution.py:51
  97.2 0.0 copy-done.1
  97.2 0.0 copy-done.5
  97.2 8.3 %fusion.6 = bf16[2,4096,128]{2,1,0:T(8,128)(2,1)S(1)} fusion(f32[2,64,4096]{2,1,0:T(8,128)} %all-gather.2.cloned.1.call-done, f32[128]{0:T(128)S(1)} %copy-done.5, f32[64,128]{1,0:T(8,128)S(1)} %copy-done.1), kind=kOutput, calls=%fused_computation.8 | convolution fusion | flops 807403520 | bytes 4227584 | tf_op jit(solution)/shard_map/tfp,fk->tpk/dot_general | solution.py:49
  105.5 0.0 copy-done
  105.5 9.0 %fusion.7 = f32[2,128]{1,0:T(2,128)S(1)} fusion(f32[2,1024]{1,0:T(2,128)S(1)} %compare_convert_fusion, bf16[2,4096,128]{2,1,0:T(8,128)(2,1)S(1)} %fusion.6, bf16[128,1024]{1,0:T(8,128)(2,1)S(1)} %copy-done, s32[1024]{0:T(1024)S(1)} %broadcast_subtract_fusion), kind=kOutput, calls=%fused_computation.9 | convolution fusion | flops 4313972736 | bytes 2372608 | tf_op jit(solution)/shard_map/tpj,js->tps/dot_general | solution.py:58
  114.6 3.8 %psum.7 = f32[2,128]{1,0:T(2,128)S(1)} all-reduce(f32[2,128]{1,0:T(2,128)S(1)} %fusion.7), channel_id=1, replica_groups=mesh['date'=16,'trade'=16,'path'=2] {'path'}, use_global_device_ids=true, to_apply=%region_4.5 | all-reduce | flops 256 | bytes 2048 | tf_op jit(solution)/shard_map/psum | solution.py:60
  118.3 0.6 broadcast_multiply_fusion
  (5 shorter events, 0.0 us)
Async XLA Ops:
  6.5 99.0 %copy-start = (bf16[128,1024]{1,0:T(8,128)(2,1)S(1)}, bf16[128,1024]{1,0:T(8,128)(2,1)}, u32[]{:S(2)}) copy-start(bf16[128,1024]{1,0:T(8,128)(2,1)} %param.17) | copy-start | bytes 786436
  6.5 45.9 %copy-start.4 = (f32[64]{0:T(128)S(1)}, f32[64]{0:T(128)}, u32[]{:S(2)}) copy-start(f32[64]{0:T(128)} %param.14) | copy-start | bytes 772
  6.5 46.7 %copy-start.3 = (s32[1024]{0:T(1024)S(1)}, s32[1024]{0:T(1024)}, u32[]{:S(2)}) copy-start(s32[1024]{0:T(1024)} %param.19) | copy-start | bytes 12292
  6.5 46.7 %copy-start.2 = (s32[1024]{0:T(1024)S(1)}, s32[1024]{0:T(1024)}, u32[]{:S(2)}) copy-start(s32[1024]{0:T(1024)} %param.18) | copy-start | bytes 12292
  6.5 90.6 %copy-start.1 = (f32[64,128]{1,0:T(8,128)S(1)}, f32[64,128]{1,0:T(8,128)}, u32[]{:S(2)}) copy-start(f32[64,128]{1,0:T(8,128)} %param.15) | copy-start | bytes 98308
  6.5 90.6 %copy-start.5 = (f32[128]{0:T(128)S(1)}, f32[128]{0:T(128)}, u32[]{:S(2)}) copy-start(f32[128]{0:T(128)} %param.16) | copy-start | bytes 1540
  6.6 90.6 %all-gather.2.cloned.1.call-start = ((), (), s32[]{:S(2)}) async-start(), calls=%async_computation | async-start | bytes 2228224 | tf_op jit(solution)/shard_map/all_gather | solution.py:51
Sparse Core Ops, SparseCore 0:
  53.3 43.8 all-gather.1
where the time goes:
time: 126 us
  blocking collectives  47.7 us (38%)
  waiting for transfers between devices  43.9 us (35%)
  matrix products  18.4 us (15%)
  between operations  13.5 us (11%)
  other arithmetic  2.22 us (2%)
    all_gather x1, blocking collectives, entering(): gathered = lax.all_gather(array.astype(jnp.bfloat16), axis)  43.9 us
    all_gather x1, waiting for transfers between devices, shards(): lax.all_gather(states, 'trade', axis=2, tiled=True)  43.9 us
    dot_general x1, matrix products, shards(): jnp.einsum('tpj,js->tps', value, member, preferred_element_type=jnp.float32)  9.03 us
    dot_general x1, matrix products, shards(): jnp.einsum('tfp,fk->tpk', lax.all_gather(states, 'trade', axis=2, tiled=T...  8.32 us
    psum x1, blocking collectives, shards(): summed = lax.psum(total, 'path')  3.79 us
  transfers between devices with their start and end apart: 1, of which 1 were waited for; matrix products, arithmetic and copies ran while one was open for 0% of the time, Pallas kernels for 0%

commit v1 on v0

--- a/solution.py
+++ b/solution.py
@@ -46,12 +46,21 @@
     empty = jnp.zeros_like(own_local[-1])
     prior = entering(own_local[-1], "date", add_pair, empty)
     states = start_state[None, :, None] + prior[None] + own_local
-    pre = jnp.einsum(
-        "tfp,fk->tpk",
-        lax.all_gather(states, "trade", axis=2, tiled=True),
-        basis_map,
-        precision=lax.Precision.HIGHEST,
-    )
+    ways, here, turn = (lax.axis_size("trade"), lax.axis_index("trade"), states.shape[2])
+    earlier_2, later_2 = ([], [])
+    going_up = going_down = states
+    for far in range(ways // 2 + 1):
+        earlier_2.append(
+            jnp.einsum("tfp,fk->tpk", going_up, basis_map, precision=lax.Precision.HIGHEST)
+        )
+        if 0 < far < ways - ways // 2:
+            later_2.append(
+                jnp.einsum("tfp,fk->tpk", going_down, basis_map, precision=lax.Precision.HIGHEST)
+            )
+        going_up = lax.ppermute(going_up, "trade", [(d, (d + 1) % ways) for d in range(ways)])
+        going_down = lax.ppermute(going_down, "trade", [(d, (d - 1) % ways) for d in range(ways)])
+    line = jnp.concatenate([*earlier_2[::-1], *later_2], axis=1)
+    pre = jnp.roll(line, (here - ways // 2) * earlier_2[0].shape[1], axis=1)
     basis = jnp.tanh(pre + basis_bias[None, None, :]).astype(jnp.bfloat16)
     value = jnp.einsum("tpk,kj->tpj", basis, coef, preferred_element_type=jnp.float32)
     value = (value * alive[:, None, :]).astype(jnp.bfloat16)

time: 126 us -> 154 us (1.22)
  the two profiles are of different devices: /device:TPU:1 before, /device:TPU:32 now
where the time goes in v1:
time: 154 us; the launch traced here: 153 us
  blocking collectives  54.8 us (36%)
  matrix products  40.1 us (26%)
  waiting for transfers between devices  22.6 us (15%)
  starting transfers between devices  20.8 us (14%)
  local copies, waits for them, and re-layouts  11.5 us (7%)
  other arithmetic  3.58 us (2%)
    all_gather x1, blocking collectives, entering(): gathered = lax.all_gather(array.astype(jnp.bfloat16), axis)  49.8 us
    ppermute x8, waiting for transfers between devices, shards(): lax.ppermute(going_up, 'trade', [(d, (d + 1) % ways) for d in range(ways)])  22.6 us
    ppermute x7, starting transfers between devices, shards(): lax.ppermute(going_down, 'trade', [(d, (d - 1) % ways) for d in range(way...  20.7 us
    dot_general x9, matrix products, shards(): jnp.einsum('tfp,fk->tpk', going_up, basis_map, precision=lax.Precision.HI...  18.5 us
    dot_general x1, matrix products, shards(): jnp.einsum('tpj,js->tps', value, member, preferred_element_type=jnp.float32)  11.4 us
    unnamed x21, local copies, waits for them, and re-layouts  10.8 us
    dot_general x7, matrix products, shards(): jnp.einsum('tfp,fk->tpk', going_down, basis_map, precision=lax.Precision....  9.13 us
    psum x1, blocking collectives, shards(): summed = lax.psum(total, 'path')  4.94 us
  transfers between devices with their start and end apart: 15, of which 8 were waited for; matrix products, arithmetic and copies ran while one was open for 18% of the time, Pallas kernels for 0%

profile of v1, /device:TPU:32, one launch (start us, length us, event | category | flops | bytes accessed | tf_op | source)
XLA Modules:
  0.0 153.4 jit_solution(4039722062248073170)
XLA Ops:
  0.7 1.0 fusion.8
  1.9 49.8 %all_gather.4 = bf16[16,64,256]{2,1,0:T(8,128)(2,1)S(1)} all-gather(bf16[1,64,256]{2,1,0:T(8,128)(2,1)S(1)} %slice.7), channel_id=1, replica_groups=mesh['date'=16,'trade'=16,'path'=2] {'date'}, dimensions={0}, use_global_device_ids=true | all-gather | bytes 557056 | tf_op jit(solution)/shard_map/all_gather | solution.py:11
  51.7 0.7 broadcast_add_fusion.1
  52.5 5.6 %collective-permute-done = f32[2,64,256]{2,1,0:T(8,128)S(1)} collective-permute-done((f32[2,64,256]{2,1,0:T(8,128)S(1)}, f32[2,64,256]{2,1,0:T(8,128)S(1)}, u32[]{:S(2)}, u32[]{:S(2)}) %collective-permute-start) | collective-permute-done | bytes 131104 | tf_op jit(solution)/shard_map/ppermute | solution.py:60
  58.1 3.0 %collective-permute-start.8 = (f32[2,64,256]{2,1,0:T(8,128)S(1)}, f32[2,64,256]{2,1,0:T(8,128)S(1)}, u32[]{:S(2)}, u32[]{:S(2)}) collective-permute-start(f32[2,64,256]{2,1,0:T(8,128)S(1)} %broadcast_add_fusion), channel_id=1, source_target_pairs={{0,30},{2,0},{4,2},{6,4},{8,6},{10,8},{12,10},{14,12},{16,14},{18,... | collective-permute-start | bytes 393224 | tf_op jit(solution)/shard_map/ppermute | solution.py:61
  61.0 2.6 %collective-permute-done.1 = f32[2,64,256]{2,1,0:T(8,128)S(1)} collective-permute-done((f32[2,64,256]{2,1,0:T(8,128)S(1)}, f32[2,64,256]{2,1,0:T(8,128)S(1)}, u32[]{:S(2)}, u32[]{:S(2)}) %collective-permute-start.1) | collective-permute-done | bytes 131104 | tf_op jit(solution)/shard_map/ppermute | solution.py:60
  63.7 3.0 %collective-permute-start.9 = (f32[2,64,256]{2,1,0:T(8,128)S(1)}, f32[2,64,256]{2,1,0:T(8,128)S(1)}, u32[]{:S(2)}, u32[]{:S(2)}) collective-permute-start(f32[2,64,256]{2,1,0:T(8,128)S(1)} %collective-permute-done.8), channel_id=1, source_target_pairs={{0,30},{2,0},{4,2},{6,4},{8,6},{10,8},{12,10},{14,12},{16,14},{18,... | collective-permute-start | bytes 393224 | tf_op jit(solution)/shard_map/ppermute | solution.py:61
  66.7 2.6 %collective-permute-done.2 = f32[2,64,256]{2,1,0:T(8,128)S(1)} collective-permute-done((f32[2,64,256]{2,1,0:T(8,128)S(1)}, f32[2,64,256]{2,1,0:T(8,128)S(1)}, u32[]{:S(2)}, u32[]{:S(2)}) %collective-permute-start.2) | collective-permute-done | bytes 131104 | tf_op jit(solution)/shard_map/ppermute | solution.py:60
  69.3 3.0 %collective-permute-start.10 = (f32[2,64,256]{2,1,0:T(8,128)S(1)}, f32[2,64,256]{2,1,0:T(8,128)S(1)}, u32[]{:S(2)}, u32[]{:S(2)}) collective-permute-start(f32[2,64,256]{2,1,0:T(8,128)S(1)} %collective-permute-done.9), channel_id=1, source_target_pairs={{0,30},{2,0},{4,2},{6,4},{8,6},{10,8},{12,10},{14,12},{16,14},{18,... | collective-permute-start | bytes 393224 | tf_op jit(solution)/shard_map/ppermute | solution.py:61
  72.3 2.6 %collective-permute-done.3 = f32[2,64,256]{2,1,0:T(8,128)S(1)} collective-permute-done((f32[2,64,256]{2,1,0:T(8,128)S(1)}, f32[2,64,256]{2,1,0:T(8,128)S(1)}, u32[]{:S(2)}, u32[]{:S(2)}) %collective-permute-start.3) | collective-permute-done | bytes 131104 | tf_op jit(solution)/shard_map/ppermute | solution.py:60
  74.9 3.0 %collective-permute-start.11 = (f32[2,64,256]{2,1,0:T(8,128)S(1)}, f32[2,64,256]{2,1,0:T(8,128)S(1)}, u32[]{:S(2)}, u32[]{:S(2)}) collective-permute-start(f32[2,64,256]{2,1,0:T(8,128)S(1)} %collective-permute-done.10), channel_id=1, source_target_pairs={{0,30},{2,0},{4,2},{6,4},{8,6},{10,8},{12,10},{14,12},{16,14},{18,... | collective-permute-start | bytes 393224 | tf_op jit(solution)/shard_map/ppermute | solution.py:61
  77.9 2.6 %collective-permute-done.4 = f32[2,64,256]{2,1,0:T(8,128)S(1)} collective-permute-done((f32[2,64,256]{2,1,0:T(8,128)S(1)}, f32[2,64,256]{2,1,0:T(8,128)S(1)}, u32[]{:S(2)}, u32[]{:S(2)}) %collective-permute-start.4) | collective-permute-done | bytes 131104 | tf_op jit(solution)/shard_map/ppermute | solution.py:60
  80.5 3.0 %collective-permute-start.12 = (f32[2,64,256]{2,1,0:T(8,128)S(1)}, f32[2,64,256]{2,1,0:T(8,128)S(1)}, u32[]{:S(2)}, u32[]{:S(2)}) collective-permute-start(f32[2,64,256]{2,1,0:T(8,128)S(1)} %collective-permute-done.11), channel_id=1, source_target_pairs={{0,30},{2,0},{4,2},{6,4},{8,6},{10,8},{12,10},{14,12},{16,14},{18,... | collective-permute-start | bytes 393224 | tf_op jit(solution)/shard_map/ppermute | solution.py:61
  83.5 2.6 %collective-permute-done.5 = f32[2,64,256]{2,1,0:T(8,128)S(1)} collective-permute-done((f32[2,64,256]{2,1,0:T(8,128)S(1)}, f32[2,64,256]{2,1,0:T(8,128)S(1)}, u32[]{:S(2)}, u32[]{:S(2)}) %collective-permute-start.5) | collective-permute-done | bytes 131104 | tf_op jit(solution)/shard_map/ppermute | solution.py:60
  86.1 0.8 compare_convert_fusion
  86.9 3.0 %collective-permute-start.13 = (f32[2,64,256]{2,1,0:T(8,128)S(1)}, f32[2,64,256]{2,1,0:T(8,128)S(1)}, u32[]{:S(2)}, u32[]{:S(2)}) collective-permute-start(f32[2,64,256]{2,1,0:T(8,128)S(1)} %collective-permute-done.12), channel_id=1, source_target_pairs={{0,30},{2,0},{4,2},{6,4},{8,6},{10,8},{12,10},{14,12},{16,14},{18,... | collective-permute-start | bytes 393224 | tf_op jit(solution)/shard_map/ppermute | solution.py:61
  89.8 1.9 %collective-permute-done.6 = f32[2,64,256]{2,1,0:T(8,128)S(1)} collective-permute-done((f32[2,64,256]{2,1,0:T(8,128)S(1)}, f32[2,64,256]{2,1,0:T(8,128)S(1)}, u32[]{:S(2)}, u32[]{:S(2)}) %collective-permute-start.6) | collective-permute-done | bytes 131104 | tf_op jit(solution)/shard_map/ppermute | solution.py:60
  92.4 3.0 %collective-permute-start.14 = (f32[2,64,256]{2,1,0:T(8,128)S(1)}, f32[2,64,256]{2,1,0:T(8,128)S(1)}, u32[]{:S(2)}, u32[]{:S(2)}) collective-permute-start(f32[2,64,256]{2,1,0:T(8,128)S(1)} %collective-permute-done.13), channel_id=1, source_target_pairs={{0,30},{2,0},{4,2},{6,4},{8,6},{10,8},{12,10},{14,12},{16,14},{18,... | collective-permute-start | bytes 393224 | tf_op jit(solution)/shard_map/ppermute | solution.py:61
  95.4 1.9 %collective-permute-done.7 = f32[2,64,256]{2,1,0:T(8,128)S(1)} collective-permute-done((f32[2,64,256]{2,1,0:T(8,128)S(1)}, f32[2,64,256]{2,1,0:T(8,128)S(1)}, u32[]{:S(2)}, u32[]{:S(2)}) %collective-permute-start.7) | collective-permute-done | bytes 131104 | tf_op jit(solution)/shard_map/ppermute | solution.py:60
  97.3 2.1 %constant_dynamic-update-slice_fusion.31 = (f32[2,8192,128]{2,1,0:T(8,128)}, f32[2,256,128]{2,1,0:T(8,128)S(1)}) fusion(f32[2,64,256]{2,1,0:T(8,128)S(1)} %collective-permute-done.7, f32[64,128]{1,0:T(8,128)} %param.15), kind=kOutput, calls=%fused_computation.46 | convolution fusion | flops 50331648 | bytes 688128 | tf_op jit(solution)/shard_map/tfp,fk->tpk/dot_general | solution.py:54
  99.4 2.0 %constant_dynamic-update-slice_fusion.30 = (f32[2,8192,128]{2,1,0:T(8,128)}, f32[2,256,128]{2,1,0:T(8,128)S(1)}) fusion(f32[2,8192,128]{2,1,0:T(8,128)} %get-tuple-element.37, f32[2,64,256]{2,1,0:T(8,128)S(1)} %collective-permute-done.6, f32[64,128]{1,0:T(8,128)} %param.15), kind=kOutput, calls=%fused_computation.45 | convolution fusion | flops 50331648 | bytes 688128 | tf_op jit(solution)/shard_map/tfp,fk->tpk/dot_general | solution.py:54
  101.4 2.0 %constant_dynamic-update-slice_fusion.29 = (f32[2,8192,128]{2,1,0:T(8,128)}, f32[2,256,128]{2,1,0:T(8,128)S(1)}) fusion(f32[2,8192,128]{2,1,0:T(8,128)} %get-tuple-element.39, f32[2,64,256]{2,1,0:T(8,128)S(1)} %collective-permute-done.5, f32[64,128]{1,0:T(8,128)} %param.15), kind=kOutput, calls=%fused_computation.44 | convolution fusion | flops 50331648 | bytes 688128 | tf_op jit(solution)/shard_map/tfp,fk->tpk/dot_general | solution.py:54
  103.5 2.1 %constant_dynamic-update-slice_fusion.28 = (f32[2,8192,128]{2,1,0:T(8,128)}, f32[2,256,128]{2,1,0:T(8,128)S(1)}) fusion(f32[2,8192,128]{2,1,0:T(8,128)} %get-tuple-element.41, f32[2,64,256]{2,1,0:T(8,128)S(1)} %collective-permute-done.4, f32[64,128]{1,0:T(8,128)} %param.15), kind=kOutput, calls=%fused_computation.43 | convolution fusion | flops 50331648 | bytes 688128 | tf_op jit(solution)/shard_map/tfp,fk->tpk/dot_general | solution.py:54
  105.5 2.1 %constant_dynamic-update-slice_fusion.27 = (f32[2,8192,128]{2,1,0:T(8,128)}, f32[2,256,128]{2,1,0:T(8,128)S(1)}) fusion(f32[2,8192,128]{2,1,0:T(8,128)} %get-tuple-element.43, f32[2,64,256]{2,1,0:T(8,128)S(1)} %collective-permute-done.3, f32[64,128]{1,0:T(8,128)} %param.15), kind=kOutput, calls=%fused_computation.42 | convolution fusion | flops 50331648 | bytes 688128 | tf_op jit(solution)/shard_map/tfp,fk->tpk/dot_general | solution.py:54
  107.6 2.1 %constant_dynamic-update-slice_fusion.26 = (f32[2,8192,128]{2,1,0:T(8,128)}, f32[2,256,128]{2,1,0:T(8,128)S(1)}) fusion(f32[2,8192,128]{2,1,0:T(8,128)} %get-tuple-element.45, f32[2,64,256]{2,1,0:T(8,128)S(1)} %collective-permute-done.2, f32[64,128]{1,0:T(8,128)} %param.15), kind=kOutput, calls=%fused_computation.41 | convolution fusion | flops 50331648 | bytes 688128 | tf_op jit(solution)/shard_map/tfp,fk->tpk/dot_general | solution.py:54
  109.7 2.1 %constant_dynamic-update-slice_fusion.25 = (f32[2,8192,128]{2,1,0:T(8,128)}, f32[2,256,128]{2,1,0:T(8,128)S(1)}) fusion(f32[2,8192,128]{2,1,0:T(8,128)} %get-tuple-element.47, f32[2,64,256]{2,1,0:T(8,128)S(1)} %collective-permute-done.1, f32[64,128]{1,0:T(8,128)} %param.15), kind=kOutput, calls=%fused_computation.40 | convolution fusion | flops 50331648 | bytes 688128 | tf_op jit(solution)/shard_map/tfp,fk->tpk/dot_general | solution.py:54
  111.7 2.1 %constant_dynamic-update-slice_fusion.24 = (f32[2,8192,128]{2,1,0:T(8,128)}, f32[2,256,128]{2,1,0:T(8,128)S(1)}) fusion(f32[2,8192,128]{2,1,0:T(8,128)} %get-tuple-element.49, f32[2,64,256]{2,1,0:T(8,128)S(1)} %collective-permute-done, f32[64,128]{1,0:T(8,128)} %param.15), kind=kOutput, calls=%fused_computation.39 | convolution fusion | flops 50331648 | bytes 688128 | tf_op jit(solution)/shard_map/tfp,fk->tpk/dot_general | solution.py:54
  113.8 2.1 %constant_dynamic-update-slice_fusion.23 = (f32[2,8192,128]{2,1,0:T(8,128)}, f32[2,256,128]{2,1,0:T(8,128)S(1)}) fusion(f32[2,8192,128]{2,1,0:T(8,128)} %get-tuple-element.51, f32[2,64,256]{2,1,0:T(8,128)S(1)} %broadcast_add_fusion, f32[64,128]{1,0:T(8,128)} %param.15), kind=kOutput, calls=%fused_computation.38 | convolution fusion | flops 50331648 | bytes 688128 | tf_op jit(solution)/shard_map/tfp,fk->tpk/dot_general | solution.py:54
  115.8 1.3 constant_dynamic-update-slice_fusion.22
  117.1 1.3 constant_dynamic-update-slice_fusion.21
  118.4 1.3 constant_dynamic-update-slice_fusion.20
  119.8 1.3 constant_dynamic-update-slice_fusion.19
  121.1 1.3 constant_dynamic-update-slice_fusion.18
  122.4 1.3 constant_dynamic-update-slice_fusion.17
  123.7 1.3 constant_dynamic-update-slice_fusion.16
  125.0 0.7 constant_dynamic-update-slice_fusion.15
  125.7 0.7 constant_dynamic-update-slice_fusion.14
  127.8 0.7 constant_dynamic-update-slice_fusion.11
  128.5 0.7 constant_dynamic-update-slice_fusion.10
  130.0 0.7 constant_dynamic-update-slice_fusion.8
  130.7 0.7 constant_dynamic-update-slice_fusion.7
  131.4 0.7 constant_dynamic-update-slice_fusion.6
  133.6 0.7 constant_dynamic-update-slice_fusion.3
  134.3 0.7 constant_dynamic-update-slice_fusion.2
  135.0 0.7 constant_dynamic-update-slice_fusion.1
  135.8 0.7 constant_dynamic-update-slice_fusion
  136.5 11.4 %fusion.7 = f32[2,128]{1,0:T(2,128)S(1)} fusion(f32[2,1024]{1,0:T(2,128)S(1)} %compare_convert_fusion, f32[2,8192,128]{2,1,0:T(8,128)} %constant_dynamic-update-slice_fusion, s32[]{:T(128)S(6)} %select_n.18, f32[128]{0:T(128)S(1)} %copy-done.2, bf16[128,1024]{1,0:T(8,128)(2,1)S(1)} %copy-done, s32[1024]{0:T(1024)S(1)} %broadcast_subtract_fusion), kind=kOutput, calls=%fused_computation.8 | convolution fusion | flops 4316069888 | bytes 4470276 | tf_op jit(solution)/shard_map/tpj,js->tps/dot_general | solution.py:67
  147.9 4.9 %psum.7 = f32[2,128]{1,0:T(2,128)S(1)} all-reduce(f32[2,128]{1,0:T(2,128)S(1)} %fusion.7), channel_id=1, replica_groups=mesh['date'=16,'trade'=16,'path'=2] {'path'}, use_global_device_ids=true, to_apply=%region_4.5 | all-reduce | flops 256 | bytes 2048 | tf_op jit(solution)/shard_map/psum | solution.py:69
  (35 shorter events, 5.7 us)
Async XLA Ops:
  0.0 136.5 %copy-start = (bf16[128,1024]{1,0:T(8,128)(2,1)S(1)}, bf16[128,1024]{1,0:T(8,128)(2,1)}, u32[]{:S(2)}) copy-start(bf16[128,1024]{1,0:T(8,128)(2,1)} %param.17) | copy-start | bytes 786436
  0.0 115.8 %copy-start.1 = (f32[64,128]{1,0:T(8,128)S(1)}, f32[64,128]{1,0:T(8,128)}, u32[]{:S(2)}) copy-start(f32[64,128]{1,0:T(8,128)} %param.15) | copy-start | bytes 98308
  52.5 5.6 %collective-permute-start = (f32[2,64,256]{2,1,0:T(8,128)S(1)}, f32[2,64,256]{2,1,0:T(8,128)S(1)}, u32[]{:S(2)}, u32[]{:S(2)}) collective-permute-start(f32[2,64,256]{2,1,0:T(8,128)S(1)} %broadcast_add_fusion), channel_id=1, source_target_pairs={{0,2},{2,4},{4,6},{6,8},{8,10},{10,12},{12,14},{14,16},{16,18},{18... | collective-permute-start | bytes 393224 | tf_op jit(solution)/shard_map/ppermute | solution.py:60
  58.1 5.6 %collective-permute-start.1 = (f32[2,64,256]{2,1,0:T(8,128)S(1)}, f32[2,64,256]{2,1,0:T(8,128)S(1)}, u32[]{:S(2)}, u32[]{:S(2)}) collective-permute-start(f32[2,64,256]{2,1,0:T(8,128)S(1)} %collective-permute-done), channel_id=1, source_target_pairs={{0,2},{2,4},{4,6},{6,8},{8,10},{10,12},{12,14},{14,16},{16,18},{18... | collective-permute-start | bytes 393224 | tf_op jit(solution)/shard_map/ppermute | solution.py:60
  58.1 5.6 %collective-permute-start.8 = (f32[2,64,256]{2,1,0:T(8,128)S(1)}, f32[2,64,256]{2,1,0:T(8,128)S(1)}, u32[]{:S(2)}, u32[]{:S(2)}) collective-permute-start(f32[2,64,256]{2,1,0:T(8,128)S(1)} %broadcast_add_fusion), channel_id=1, source_target_pairs={{0,30},{2,0},{4,2},{6,4},{8,6},{10,8},{12,10},{14,12},{16,14},{18,... | collective-permute-start | bytes 393224 | tf_op jit(solution)/shard_map/ppermute | solution.py:61
  63.7 5.6 %collective-permute-start.2 = (f32[2,64,256]{2,1,0:T(8,128)S(1)}, f32[2,64,256]{2,1,0:T(8,128)S(1)}, u32[]{:S(2)}, u32[]{:S(2)}) collective-permute-start(f32[2,64,256]{2,1,0:T(8,128)S(1)} %collective-permute-done.1), channel_id=1, source_target_pairs={{0,2},{2,4},{4,6},{6,8},{8,10},{10,12},{12,14},{14,16},{16,18},{18... | collective-permute-start | bytes 393224 | tf_op jit(solution)/shard_map/ppermute | solution.py:60
  63.7 5.6 %collective-permute-start.9 = (f32[2,64,256]{2,1,0:T(8,128)S(1)}, f32[2,64,256]{2,1,0:T(8,128)S(1)}, u32[]{:S(2)}, u32[]{:S(2)}) collective-permute-start(f32[2,64,256]{2,1,0:T(8,128)S(1)} %collective-permute-done.8), channel_id=1, source_target_pairs={{0,30},{2,0},{4,2},{6,4},{8,6},{10,8},{12,10},{14,12},{16,14},{18,... | collective-permute-start | bytes 393224 | tf_op jit(solution)/shard_map/ppermute | solution.py:61
  69.3 5.6 %collective-permute-start.3 = (f32[2,64,256]{2,1,0:T(8,128)S(1)}, f32[2,64,256]{2,1,0:T(8,128)S(1)}, u32[]{:S(2)}, u32[]{:S(2)}) collective-permute-start(f32[2,64,256]{2,1,0:T(8,128)S(1)} %collective-permute-done.2), channel_id=1, source_target_pairs={{0,2},{2,4},{4,6},{6,8},{8,10},{10,12},{12,14},{14,16},{16,18},{18... | collective-permute-start | bytes 393224 | tf_op jit(solution)/shard_map/ppermute | solution.py:60
  69.3 5.6 %collective-permute-start.10 = (f32[2,64,256]{2,1,0:T(8,128)S(1)}, f32[2,64,256]{2,1,0:T(8,128)S(1)}, u32[]{:S(2)}, u32[]{:S(2)}) collective-permute-start(f32[2,64,256]{2,1,0:T(8,128)S(1)} %collective-permute-done.9), channel_id=1, source_target_pairs={{0,30},{2,0},{4,2},{6,4},{8,6},{10,8},{12,10},{14,12},{16,14},{18,... | collective-permute-start | bytes 393224 | tf_op jit(solution)/shard_map/ppermute | solution.py:61
  74.9 5.6 %collective-permute-start.4 = (f32[2,64,256]{2,1,0:T(8,128)S(1)}, f32[2,64,256]{2,1,0:T(8,128)S(1)}, u32[]{:S(2)}, u32[]{:S(2)}) collective-permute-start(f32[2,64,256]{2,1,0:T(8,128)S(1)} %collective-permute-done.3), channel_id=1, source_target_pairs={{0,2},{2,4},{4,6},{6,8},{8,10},{10,12},{12,14},{14,16},{16,18},{18... | collective-permute-start | bytes 393224 | tf_op jit(solution)/shard_map/ppermute | solution.py:60
  74.9 5.6 %collective-permute-start.11 = (f32[2,64,256]{2,1,0:T(8,128)S(1)}, f32[2,64,256]{2,1,0:T(8,128)S(1)}, u32[]{:S(2)}, u32[]{:S(2)}) collective-permute-start(f32[2,64,256]{2,1,0:T(8,128)S(1)} %collective-permute-done.10), channel_id=1, source_target_pairs={{0,30},{2,0},{4,2},{6,4},{8,6},{10,8},{12,10},{14,12},{16,14},{18,... | collective-permute-start | bytes 393224 | tf_op jit(solution)/shard_map/ppermute | solution.py:61
  80.5 5.6 %collective-permute-start.5 = (f32[2,64,256]{2,1,0:T(8,128)S(1)}, f32[2,64,256]{2,1,0:T(8,128)S(1)}, u32[]{:S(2)}, u32[]{:S(2)}) collective-permute-start(f32[2,64,256]{2,1,0:T(8,128)S(1)} %collective-permute-done.4), channel_id=1, source_target_pairs={{0,2},{2,4},{4,6},{6,8},{8,10},{10,12},{12,14},{14,16},{16,18},{18... | collective-permute-start | bytes 393224 | tf_op jit(solution)/shard_map/ppermute | solution.py:60
  80.5 6.4 %collective-permute-start.12 = (f32[2,64,256]{2,1,0:T(8,128)S(1)}, f32[2,64,256]{2,1,0:T(8,128)S(1)}, u32[]{:S(2)}, u32[]{:S(2)}) collective-permute-start(f32[2,64,256]{2,1,0:T(8,128)S(1)} %collective-permute-done.11), channel_id=1, source_target_pairs={{0,30},{2,0},{4,2},{6,4},{8,6},{10,8},{12,10},{14,12},{16,14},{18,... | collective-permute-start | bytes 393224 | tf_op jit(solution)/shard_map/ppermute | solution.py:61
  86.1 5.6 %collective-permute-start.6 = (f32[2,64,256]{2,1,0:T(8,128)S(1)}, f32[2,64,256]{2,1,0:T(8,128)S(1)}, u32[]{:S(2)}, u32[]{:S(2)}) collective-permute-start(f32[2,64,256]{2,1,0:T(8,128)S(1)} %collective-permute-done.5), channel_id=1, source_target_pairs={{0,2},{2,4},{4,6},{6,8},{8,10},{10,12},{12,14},{14,16},{16,18},{18... | collective-permute-start | bytes 393224 | tf_op jit(solution)/shard_map/ppermute | solution.py:60
  86.9 5.5 %collective-permute-start.13 = (f32[2,64,256]{2,1,0:T(8,128)S(1)}, f32[2,64,256]{2,1,0:T(8,128)S(1)}, u32[]{:S(2)}, u32[]{:S(2)}) collective-permute-start(f32[2,64,256]{2,1,0:T(8,128)S(1)} %collective-permute-done.12), channel_id=1, source_target_pairs={{0,30},{2,0},{4,2},{6,4},{8,6},{10,8},{12,10},{14,12},{16,14},{18,... | collective-permute-start | bytes 393224 | tf_op jit(solution)/shard_map/ppermute | solution.py:61
  91.7 5.6 %collective-permute-start.7 = (f32[2,64,256]{2,1,0:T(8,128)S(1)}, f32[2,64,256]{2,1,0:T(8,128)S(1)}, u32[]{:S(2)}, u32[]{:S(2)}) collective-permute-start(f32[2,64,256]{2,1,0:T(8,128)S(1)} %collective-permute-done.6), channel_id=1, source_target_pairs={{0,2},{2,4},{4,6},{6,8},{8,10},{10,12},{12,14},{14,16},{16,18},{18... | collective-permute-start | bytes 393224 | tf_op jit(solution)/shard_map/ppermute | solution.py:60
  92.4 31.3 %collective-permute-start.14 = (f32[2,64,256]{2,1,0:T(8,128)S(1)}, f32[2,64,256]{2,1,0:T(8,128)S(1)}, u32[]{:S(2)}, u32[]{:S(2)}) collective-permute-start(f32[2,64,256]{2,1,0:T(8,128)S(1)} %collective-permute-done.13), channel_id=1, source_target_pairs={{0,30},{2,0},{4,2},{6,4},{8,6},{10,8},{12,10},{14,12},{16,14},{18,... | collective-permute-start | bytes 393224 | tf_op jit(solution)/shard_map/ppermute | solution.py:61
  105.5 31.0 %copy-start.2 = (f32[128]{0:T(128)S(1)}, f32[128]{0:T(128)}, u32[]{:S(2)}) copy-start(f32[128]{0:T(128)} %param.16) | copy-start | bytes 1540
